TPU v7x, 512 devices: a whole 4x4x16 slice. The times are simulated.
512 devices in a mesh: seq: 64 (over z, x), head: 8 (over y, core).
Axes of the slice: x: 4, y: 4, z: 16, core: 2. Of those that a mesh axis runs over, the one named last changes fastest.
Arguments:
- hidden: bfloat16 [32768, 4096], P('seq'), may hold values from -6 to 6
- steer: bfloat16 [4096], replicated, may hold values from -4 to 4
- w_x: bfloat16 [4096, 4096], P('seq', 'head'), may hold values from -0.09375 to 0.09375
- w_z: bfloat16 [4096, 4096], P('seq', 'head'), may hold values from -0.09375 to 0.09375
- w_shared: bfloat16 [4096, 320], P(('seq', 'head')), may hold values from -0.09375 to 0.09375
- conv_x: float32 [4, 4096], P(None, 'head'), may hold values from -3 to 3
- conv_shared: float32 [4, 256], replicated, may hold values from -3 to 3
- dt_bias: float32 [64], P('head'), may hold values from -7 to 0
- decay_rate: float32 [64], P('head'), may hold values from 0.01 to 16
- skip: float32 [64], P('head'), may hold values from 0.5 to 1.5
- norm_gain: float32 [4096], P('head'), may hold values from 0.5 to 1.5
Outputs:
- mixed: bfloat16 [32768, 4096], P('seq', 'head')
All inputs are finite; a program needn't handle non-finite values.
Results may differ from a plain program's by a relative error of at most 0.0095.
Values may be sent and summed in bfloat16 or wider, within the bound.
No kernel may reach another device: no remote copies, remote signals or barrier semaphores. Data moves between devices by JAX's collectives and lax.ppermute only.
A program may use at most 128 MiB of HBM per device.

v0:
```python
import jax
import jax.numpy as jnp
from jax import lax
from jax.sharding import PartitionSpec as P

STATE = 128
CONV = 4
SPAN = 128
highest = lax.Precision.HIGHEST


def shifted(block, axis, distance):
    devices = range(lax.axis_size(axis))
    route = [(i - distance, i) for i in devices if i - distance in devices]
    return lax.ppermute(block, axis, route)


def carried_in(shard, axis, combine, identity):
    count, position = (lax.axis_size(axis), lax.axis_index(axis))
    everything = jax.tree.map(
        lambda part, kind: lax.all_gather(part.astype(kind), axis),
        shard,
        (jnp.bfloat16, jnp.bfloat16),
    )
    start = jax.tree.map(
        lambda part, zero: jnp.broadcast_to(jnp.asarray(zero, part.dtype), part.shape),
        shard,
        identity,
    )

    def step(k, before):
        reached = k < position
        new = combine(
            before, jax.tree.map(lambda part, own: part[k].astype(own.dtype), everything, shard)
        )
        return jax.tree.map(lambda a, b: jnp.where(reached, a, b), new, before)

    return lax.fori_loop(0, count, step, start)


def conv_valid(extended, weights):
    taps = weights.shape[0]
    count = extended.shape[0] - taps + 1
    values = extended.astype(jnp.float32)
    total = jnp.zeros((count, extended.shape[1]), jnp.float32)
    for k in range(taps):
        total = total + values[k : k + count] * weights[k]
    return total


def span_pass(inputs, steps, logs, in_map, out_map, start):
    blocks = inputs.shape[0] // SPAN
    heads = inputs.shape[1]
    width = inputs.shape[2]
    index = jnp.arange(SPAN)
    lower = index[:, None] >= index[None, :]

    def advance(state, block):
        xblock, dblock, lblock, bblock, cblock = block
        cums = jnp.cumsum(lblock, axis=0)
        gram = jnp.dot(cblock, bblock.T, precision=highest)
        diff = cums[:, None, :] - cums[None, :, :]
        decay = jnp.exp(jnp.where(lower[:, :, None], diff, -1e30))
        weights = gram[:, :, None] * decay * dblock[None, :, :]
        within = jnp.einsum("ijh,jhp->ihp", weights, xblock, precision=highest)
        carried = (
            jnp.einsum("in,hpn->ihp", cblock, state, precision=highest) * jnp.exp(cums)[:, :, None]
        )
        tail = jnp.exp(cums[-1][None, :] - cums) * dblock
        fresh = jnp.einsum("jh,jhp,jn->hpn", tail, xblock, bblock, precision=highest)
        state = jnp.exp(cums[-1])[:, None, None] * state + fresh
        return (state, within + carried)

    final, outs = lax.scan(
        advance,
        start,
        (
            inputs.reshape(blocks, SPAN, heads, width),
            steps.reshape(blocks, SPAN, heads),
            logs.reshape(blocks, SPAN, heads),
            in_map.reshape(blocks, SPAN, in_map.shape[1]),
            out_map.reshape(blocks, SPAN, out_map.shape[1]),
        ),
    )
    return (outs.reshape(-1, heads, width), final)


def combine_states(earlier, later):
    return (earlier[0] + later[0], jnp.exp(later[0])[:, None, None] * earlier[1] + later[1])


def on_device(
    hidden, steer, w_x, w_z, w_shared, conv_x, conv_shared, dt_bias, decay_rate, skip, norm_gain
):
    rows = hidden.shape[0]
    edge = CONV - 1
    head_count = dt_bias.shape[0]
    width = w_x.shape[1]
    head_index = lax.axis_index("head")
    steered = (hidden.astype(jnp.float32) + steer.astype(jnp.float32)).astype(jnp.bfloat16)
    columns = steered
    x_sum = jnp.dot(
        columns, lax.all_gather(w_x, "seq", axis=0, tiled=True), preferred_element_type=jnp.float32
    )
    z_sum = jnp.dot(
        columns, lax.all_gather(w_z, "seq", axis=0, tiled=True), preferred_element_type=jnp.float32
    )
    columns = steered
    shared = jnp.dot(
        columns,
        lax.all_gather(w_shared, ("seq", "head"), axis=0, tiled=True),
        preferred_element_type=jnp.float32,
    )
    x_raw = x_sum.astype(jnp.bfloat16)
    z_raw = z_sum.astype(jnp.bfloat16)
    b_raw = shared[:, : 2 * STATE].astype(jnp.bfloat16)
    dt_raw = shared[:, 2 * STATE :]
    x_prev, b_prev = shifted((x_raw[rows - edge :], b_raw[rows - edge :]), "seq", 1)
    x_ext = jnp.concatenate([x_prev, x_raw], axis=0)
    b_ext = jnp.concatenate([b_prev, b_raw], axis=0)
    x_conv = jax.nn.silu(conv_valid(x_ext, conv_x)).astype(jnp.bfloat16)
    b_conv = jax.nn.silu(conv_valid(b_ext, conv_shared)).astype(jnp.bfloat16)
    in_map = b_conv[:, :STATE].astype(jnp.float32)
    out_map = b_conv[:, STATE:].astype(jnp.float32)
    dt_mine = lax.dynamic_slice_in_dim(dt_raw, head_index * head_count, head_count, 1)
    steps = jax.nn.softplus(dt_mine + dt_bias)
    logs = -steps * decay_rate
    inputs = x_conv.astype(jnp.float32).reshape(rows, head_count, width // head_count)
    start = jnp.zeros((head_count, width // head_count, STATE), jnp.float32)
    heads_out, final = span_pass(inputs, steps, logs, in_map, out_map, start)
    total_log = jnp.sum(logs, axis=0)
    identity = (jnp.zeros_like(total_log), jnp.zeros_like(final))
    log_in, state_in = carried_in((total_log, final), "seq", combine_states, identity)
    running = jnp.cumsum(logs, axis=0)
    incoming = (
        jnp.einsum("tn,hpn->thp", out_map, state_in, precision=highest)
        * jnp.exp(running)[:, :, None]
    )
    heads_out = heads_out + incoming + skip[None, :, None] * inputs
    gated = heads_out.reshape(rows, width) * jax.nn.silu(z_raw.astype(jnp.float32))
    squares = lax.psum(jnp.sum(gated * gated, axis=1), "head")
    total_width = width * lax.axis_size("head")
    scale = lax.rsqrt(squares / total_width + 1e-05)
    return (gated * scale[:, None] * norm_gain).astype(jnp.bfloat16)


def solution(mesh):
    placed = (
        P("seq", None),
        P(),
        P("seq", "head"),
        P("seq", "head"),
        P(("seq", "head"), None),
        P(None, "head"),
        P(),
        P("head"),
        P("head"),
        P("head"),
        P("head"),
    )
    return jax.shard_map(
        on_device, mesh=mesh, in_specs=placed, out_specs=P("seq", "head"), check_vma=False
    )
```

profile of v0, /device:TPU:1, one launch (start us, length us, event | category | flops | bytes accessed | tf_op | source)
XLA Modules:
  0.0 753.1 jit_solution(3623105152973031940)
XLA Ops:
  10.5 203.2 %all-gather.7.cloned.1.call-done = bf16[4096,320]{1,0:T(8,128)(2,1)} async-done(((bf16[8,320]{1,0:T(8,128)(2,1)}), bf16[4096,320]{1,0:T(8,128)(2,1)}) %all-gather.7.cloned.1.call-update) | async-done | bytes 2621456 | tf_op jit(solution)/shard_map/all_gather | solution.py:111
  213.7 4.8 fusion.65
  218.6 3.2 collective-permute-start.1
  222.0 1.0 collective-permute-done.1
  223.9 125.1 %all-gather.9.cloned.1.call-done = bf16[4096,512]{1,0:T(8,128)(2,1)} async-done(((bf16[64,512]{1,0:T(8,128)(2,1)}), bf16[4096,512]{1,0:T(8,128)(2,1)}) %all-gather.9.cloned.1.call-update) | async-done | bytes 4194320 | tf_op jit(solution)/shard_map/all_gather | solution.py:103
  349.0 5.8 fusion.43
  354.8 1.7 collective-permute-start
  359.5 1.6 copy.51
  361.1 56.6 %while.27 = (s32[]{:T(128)}, f32[8,64,128]{2,1,0:T(8,128)S(1)}, f32[4,128,8,64]{1,0,3,2:T(4,128)}, f32[4,128,8]{1,2,0:T(8,128)S(1)}, f32[4,128,8]{1,2,0:T(8,128)...) while((s32[]{:T(128)}, f32[8,64,128]{2,1,0:T(8,128)S(1)}, ...), condition=%wide.region_2.3_spmd.clone, body=%wide.region_0.2_spmd.clone.sunk | while | flops 328287232 | bytes 3153220 | solution.py:74
  361.4 1.2 fusion.91
  362.6 2.1 convolution_bitcast_fusion.2
  364.9 1.2 fusion.92
  366.2 7.5 dynamic_update_slice.6
  373.8 1.5 convolution_add_fusion.2
  375.6 1.2 fusion.91
  376.8 2.1 convolution_bitcast_fusion.2
  379.1 1.2 fusion.92
  380.3 7.5 dynamic_update_slice.6
  387.9 1.5 convolution_add_fusion.2
  389.7 1.2 fusion.91
  390.9 2.1 convolution_bitcast_fusion.2
  393.2 1.2 fusion.92
  394.5 7.5 dynamic_update_slice.6
  402.1 1.5 convolution_add_fusion.2
  403.9 1.2 fusion.91
  405.1 2.1 convolution_bitcast_fusion.2
  407.4 1.2 fusion.92
  408.7 7.5 dynamic_update_slice.6
  416.2 1.5 convolution_add_fusion.2
  419.0 1.3 dynamic-slice
  421.2 114.6 %all-reduce = bf16[512]{0:T(512)(128)(2,1)S(1)} all-reduce(bf16[512]{0:T(512)(128)(2,1)S(1)} %dynamic-update-slice), channel_id=2, replica_groups=mesh['seq'=64,'head'=8] {'seq'}, use_global_device_ids=true, to_apply=%add | all-reduce | flops 512 | bytes 2048
  535.9 1.1 reduce-window.6
  537.7 1.7 reshape.83
  539.4 36.1 %all-gather.13.cloned.1.call-done = bf16[512,64,128]{2,1,0:T(8,128)(2,1)} async-done(((bf16[8,64,128]{2,1,0:T(8,128)(2,1)}), bf16[512,64,128]{2,1,0:T(8,128)(2,1)}) %all-gather.13.cloned.1.call-update) | async-done | bytes 8388624 | tf_op jit(solution)/shard_map/all_gather | solution.py:21
  575.4 67.5 %while.28 = (s32[]{:T(128)}, f32[8,64,128]{2,1,0:T(8,128)S(1)}, s32[]{:T(128)}, bf16[64,8]{1,0:T(8,128)(2,1)S(1)}, bf16[64,8,64,128]{3,2,1,0:T(8,128)(2,1)}, /*index=5*/s32[]{:T(128)}, s32[]{:T(128)}) while((s32[]{:T(128)}, f32[8,64,128]{2,1,0:T(8,128)S(1)}, s32[]{:T(128)}, bf16[64,8]{1,0:T(8,128)(2,1)S(1)}, ...), condition=%wide.region_5.6_spmd.clone, body=%wide.region_4.5_spmd.clone.sunk | while | flops 327692 | bytes 655545 | solution.py:38
  575.4 1.0 fusion.93
  576.5 1.0 fusion.93
  577.5 1.0 fusion.93
  578.6 1.0 fusion.93
  579.6 1.0 fusion.93
  580.7 1.0 fusion.93
  581.8 1.0 fusion.93
  582.8 1.0 fusion.93
  583.9 1.0 fusion.93
  590.2 1.0 fusion.93
  591.3 1.0 fusion.93
  596.5 1.0 fusion.93
  597.6 1.0 fusion.93
  602.9 1.0 fusion.93
  608.1 1.0 fusion.93
  609.2 1.0 fusion.93
  613.4 1.0 fusion.93
  614.5 1.0 fusion.93
  619.8 1.0 fusion.93
  620.8 1.0 fusion.93
  627.1 1.0 fusion.93
  628.2 1.0 fusion.93
  632.4 1.0 fusion.93
  638.7 1.0 fusion.93
  639.8 1.0 fusion.93
  642.9 1.5 fusion.42
  644.9 73.1 %all-gather.11.cloned.1.call-done = bf16[4096,512]{1,0:T(8,128)(2,1)} async-done(((bf16[64,512]{1,0:T(8,128)(2,1)}), bf16[4096,512]{1,0:T(8,128)(2,1)}) %all-gather.11.cloned.1.call-update) | async-done | bytes 4194320 | tf_op jit(solution)/shard_map/all_gather | solution.py:106
  718.0 6.1 multiply_reduce_fusion
  724.0 21.6 %psum.7 = f32[512]{0:T(512)S(1)} all-reduce(f32[512]{0:T(512)S(1)} %get-tuple-element.267), channel_id=1, replica_groups=mesh['seq'=64,'head'=8] {'head'}, use_global_device_ids=true, to_apply=%region_9.10 | all-reduce | flops 512 | bytes 4096 | tf_op jit(solution)/shard_map/psum | solution.py:141
  (197 shorter events, 54.1 us)
Async XLA Ops:
  6.5 207.2 %all-gather.7.cloned.1.call-start = ((), (), s32[]{:S(2)}) async-start(), calls=%async_computation | async-start | bytes 3151872 | tf_op jit(solution)/shard_map/all_gather | solution.py:111
  7.3 341.7 %all-gather.9.cloned.1.call-start = ((), (), s32[]{:S(2)}) async-start(), calls=%async_computation.1 | async-start | bytes 4259840 | tf_op jit(solution)/shard_map/all_gather | solution.py:103
  8.0 567.4 %all-gather.13.cloned.1.call-start = ((), (), s32[]{:S(2)}) async-start(), calls=%async_computation.3 | async-start | bytes 8519680 | tf_op jit(solution)/shard_map/all_gather | solution.py:21
  10.5 211.3 %copy-start.2 = (f32[8]{0:T(128)S(1)}, f32[8]{0:T(128)}, u32[]{:S(2)}) copy-start(f32[8]{0:T(128)} %param.23) | copy-start | bytes 100
  10.5 211.3 %copy-start.3 = (f32[8]{0:T(128)S(1)}, f32[8]{0:T(128)}, u32[]{:S(2)}) copy-start(f32[8]{0:T(128)} %param.22) | copy-start | bytes 100
  218.6 4.5 collective-permute-start.1
  223.9 132.6 %copy-start = (bf16[512,256]{0,1:T(8,128)(2,1)}, bf16[512,256]{0,1:T(8,128)(2,1)S(1)}, u32[]{:S(2)}) copy-start(bf16[512,256]{0,1:T(8,128)(2,1)S(1)} %multiply_convert_fusion.2) | copy-start | bytes 786436
  354.8 3.5 collective-permute-start
  417.7 225.2 %copy-start.4 = (f32[8]{0:T(128)S(1)}, f32[8]{0:T(128)}, u32[]{:S(2)}) copy-start(f32[8]{0:T(128)} %param.24) | copy-start | bytes 100
  418.4 299.5 %all-gather.11.cloned.1.call-start = ((), (), s32[]{:S(2)}) async-start(), calls=%async_computation.2 | async-start | bytes 4259840 | tf_op jit(solution)/shard_map/all_gather | solution.py:106
  644.8 100.8 %copy-start.1 = (f32[512]{0:T(512)S(1)}, f32[512]{0:T(512)}, u32[]{:S(2)}) copy-start(f32[512]{0:T(512)} %param.25) | copy-start | bytes 6148
Sparse Core Ops, SparseCore 0:
  11.7 201.9 all-gather.6
  216.7 132.3 all-gather.8
  418.5 156.8 all-gather.12
  578.2 139.6 all-gather.10
where the time goes:
time: 756 us; the launch traced here: 753 us
  waiting for transfers between devices  440 us (58%)
  blocking collectives  136 us (18%)
  other arithmetic  71.9 us (10%)
  matrix products  42.1 us (6%)
  local copies, waits for them, and re-layouts  41.2 us (5%)
  between operations  14 us (2%)
    all_gather x1, waiting for transfers between devices, on_device(): lax.all_gather(w_shared, ('seq', 'head'), axis=0, tiled=True)  203 us
    all_gather x1, waiting for transfers between devices, on_device(): lax.all_gather(w_x, 'seq', axis=0, tiled=True)  125 us
    unnamed x1, blocking collectives  115 us
    all_gather x1, waiting for transfers between devices, on_device(): lax.all_gather(w_z, 'seq', axis=0, tiled=True)  73.1 us
    select_n x64, other arithmetic, step(): return jax.tree.map(lambda a, b: jnp.where(reached, a, b), new, before)  64.8 us
    all_gather x1, waiting for transfers between devices, carried_in(): lax.all_gather(part.astype(kind), axis)  36.1 us
    dynamic_update_slice x4, local copies, waits for them, and re-layouts, span_pass(): lax.scan(advance, start, (inputs.reshape(blocks, SPAN, heads, width), ste...  30.1 us
    psum x1, blocking collectives, on_device(): squares = lax.psum(jnp.sum(gated * gated, axis=1), 'head')  21.6 us
  transfers between devices with their start and end apart: 6, of which 5 were waited for; matrix products, arithmetic and copies ran while one was open for 11% of the time, Pallas kernels for 0%

commit v1 on v0

--- a/solution.py
+++ b/solution.py
@@ -1,3 +1,4 @@
+import functools
 import jax
 import jax.numpy as jnp
 from jax import lax
@@ -7,6 +8,15 @@
 CONV = 4
 SPAN = 128
 highest = lax.Precision.HIGHEST
+
+
+def cut_skins(row_data, a_name):
+    moved = jnp.stack([row_data for _ in range(lax.axis_size(a_name))], 0)
+    k_now = lax.all_to_all(moved, concat_axis=0, axis_name=a_name, split_axis=0)
+    return jnp.concatenate(k_now, axis=0)
+
+
+roots_link = functools.partial(cut_skins, a_name=("seq", "head"))
 
 
 def shifted(block, axis, distance):
@@ -106,11 +116,7 @@
         columns, lax.all_gather(w_z, "seq", axis=0, tiled=True), preferred_element_type=jnp.float32
     )
     columns = steered
-    shared = jnp.dot(
-        columns,
-        lax.all_gather(w_shared, ("seq", "head"), axis=0, tiled=True),
-        preferred_element_type=jnp.float32,
-    )
+    shared = jnp.dot(columns, roots_link(w_shared), preferred_element_type=jnp.float32)
     x_raw = x_sum.astype(jnp.bfloat16)
     z_raw = z_sum.astype(jnp.bfloat16)
     b_raw = shared[:, : 2 * STATE].astype(jnp.bfloat16)

time: 756 us -> 618 us (0.82)
  waiting for transfers between devices: 440 us -> 285 us
  starting transfers between devices: 5.01 us -> 33.2 us
  matrix products: 42.1 us -> 27.7 us
    all_gather x1 -> x0, waiting for transfers between devices: 203 us -> none  [on_device(): lax.all_gather(w_shared, ('seq', 'head'), axis=0, tiled=True)]
    all_gather x1, waiting for transfers between devices: 125 us -> 175 us  [on_device(): lax.all_gather(w_x, 'seq', axis=0, tiled=True)]
    all_to_all x0 -> x1, starting transfers between devices: none -> 26.1 us  [cut_skins(): k_now = lax.all_to_all(moved, concat_axis=0, axis_name=a_name, split_axis=0)]
  transfers between devices with their start and end apart: 6 -> 6, of which waited for: 5 -> 5; matrix products, arithmetic and copies ran while one was open for 11% -> 13% of each run, Pallas kernels for 0% -> 0%
where the time goes in v1:
time: 618 us; the launch traced here: 616 us
  waiting for transfers between devices  285 us (46%)
  blocking collectives  137 us (22%)
  other arithmetic  72.9 us (12%)
  local copies, waits for them, and re-layouts  44.3 us (7%)
  starting transfers between devices  33.2 us (5%)
  matrix products  27.7 us (4%)
  between operations  14.2 us (2%)
    all_gather x1, waiting for transfers between devices, on_device(): lax.all_gather(w_x, 'seq', axis=0, tiled=True)  175 us
    unnamed x1, blocking collectives  115 us
    all_gather x1, waiting for transfers between devices, on_device(): lax.all_gather(w_z, 'seq', axis=0, tiled=True)  73.6 us
    select_n x64, other arithmetic, step(): return jax.tree.map(lambda a, b: jnp.where(reached, a, b), new, before)  64.8 us
    all_gather x1, waiting for transfers between devices, carried_in(): lax.all_gather(part.astype(kind), axis)  33.8 us
    dynamic_update_slice x4, local copies, waits for them, and re-layouts, span_pass(): lax.scan(advance, start, (inputs.reshape(blocks, SPAN, heads, width), ste...  30.1 us
    all_to_all x1, starting transfers between devices, cut_skins(): k_now = lax.all_to_all(moved, concat_axis=0, axis_name=a_name, split_axis=0)  26.1 us
    psum x1, blocking collectives, on_device(): squares = lax.psum(jnp.sum(gated * gated, axis=1), 'head')  21.6 us
  transfers between devices with their start and end apart: 6, of which 5 were waited for; matrix products, arithmetic and copies ran while one was open for 13% of the time, Pallas kernels for 0%

profile of v1, /device:TPU:1, one launch (start us, length us, event | category | flops | bytes accessed | tf_op | source)
XLA Modules:
  0.0 615.8 jit_solution(12993572222781899122)
XLA Ops:
  6.5 2.7 stack.2
  9.2 26.1 %all-to-all-start = ((bf16[512,8,320]{2,1,0:T(8,128)(2,1)}), bf16[512,8,320]{2,1,0:T(8,128)(2,1)}, u32[]{:S(2)}, u32[]{:S(2)}) async-start(bf16[512,8,320]{2,1,0:T(8,128)(2,1)} %stack.2), calls=%async_computation | async-start | bytes 6291456 | tf_op jit(solution)/shard_map/all_to_all | solution.py:15
  36.2 175.1 %all-gather.6.cloned.1.call-done = bf16[4096,512]{1,0:T(8,128)(2,1)} async-done(((bf16[64,512]{1,0:T(8,128)(2,1)}), bf16[4096,512]{1,0:T(8,128)(2,1)}) %all-gather.6.cloned.1.call-update) | async-done | bytes 4194320 | tf_op jit(solution)/shard_map/all_gather | solution.py:113
  211.3 5.8 fusion.44
  217.1 3.1 collective-permute-start
  222.1 1.6 copy.51
  223.8 4.8 fusion.66
  228.6 3.9 collective-permute-start.1
  235.5 44.9 %while.27 = (s32[]{:T(128)}, f32[8,64,128]{2,1,0:T(8,128)S(1)}, f32[4,128,8,64]{1,0,3,2:T(4,128)}, f32[4,128,8]{1,2,0:T(8,128)}, f32[4,128,8]{1,2,0:T(8,128)}, /...) while((s32[]{:T(128)}, f32[8,64,128]{2,1,0:T(8,128)S(1)}, ...), condition=%wide.region_2.3_spmd.clone, body=%wide.region_0.2_spmd.clone.sunk | while | flops 328287232 | bytes 3152684 | solution.py:84
  236.9 1.2 convolution_bitcast_fusion.2
  238.7 7.5 %dynamic_update_slice.6 = f32[4,128,8,64]{1,0,3,2:T(4,128)} dynamic-update-slice(f32[4,128,8,64]{1,0,3,2:T(4,128)} %get-tuple-element.370, f32[1,128,8,64]{1,0,3,2:T(1,128)S(1)} %bitcast.102, s32[]{:T(128)} %get-tuple-element.368, s32[]{:T(128)} %constant.68.clone.1..sunk, s32[]{:T(128)} %constant.68.clone.1..sunk, s32[]{:T(128)} %constant.68.clone.1..sunk) | dynamic-update-slice | bytes 524292 | tf_op jit(solution)/shard_map/while/body/jit(dynamic_update_index_in_dim)/dynamic_update_slice | solution.py:84
  248.1 1.2 convolution_bitcast_fusion.2
  249.9 7.5 %dynamic_update_slice.6 = f32[4,128,8,64]{1,0,3,2:T(4,128)} dynamic-update-slice(f32[4,128,8,64]{1,0,3,2:T(4,128)} %get-tuple-element.370, f32[1,128,8,64]{1,0,3,2:T(1,128)S(1)} %bitcast.102, s32[]{:T(128)} %get-tuple-element.368, s32[]{:T(128)} %constant.68.clone.1..sunk, s32[]{:T(128)} %constant.68.clone.1..sunk, s32[]{:T(128)} %constant.68.clone.1..sunk) | dynamic-update-slice | bytes 524292 | tf_op jit(solution)/shard_map/while/body/jit(dynamic_update_index_in_dim)/dynamic_update_slice | solution.py:84
  259.3 1.2 convolution_bitcast_fusion.2
  261.1 7.5 %dynamic_update_slice.6 = f32[4,128,8,64]{1,0,3,2:T(4,128)} dynamic-update-slice(f32[4,128,8,64]{1,0,3,2:T(4,128)} %get-tuple-element.370, f32[1,128,8,64]{1,0,3,2:T(1,128)S(1)} %bitcast.102, s32[]{:T(128)} %get-tuple-element.368, s32[]{:T(128)} %constant.68.clone.1..sunk, s32[]{:T(128)} %constant.68.clone.1..sunk, s32[]{:T(128)} %constant.68.clone.1..sunk) | dynamic-update-slice | bytes 524292 | tf_op jit(solution)/shard_map/while/body/jit(dynamic_update_index_in_dim)/dynamic_update_slice | solution.py:84
  270.5 1.2 convolution_bitcast_fusion.2
  272.3 7.5 %dynamic_update_slice.6 = f32[4,128,8,64]{1,0,3,2:T(4,128)} dynamic-update-slice(f32[4,128,8,64]{1,0,3,2:T(4,128)} %get-tuple-element.370, f32[1,128,8,64]{1,0,3,2:T(1,128)S(1)} %bitcast.102, s32[]{:T(128)} %get-tuple-element.368, s32[]{:T(128)} %constant.68.clone.1..sunk, s32[]{:T(128)} %constant.68.clone.1..sunk, s32[]{:T(128)} %constant.68.clone.1..sunk) | dynamic-update-slice | bytes 524292 | tf_op jit(solution)/shard_map/while/body/jit(dynamic_update_index_in_dim)/dynamic_update_slice | solution.py:84
  281.9 1.3 dynamic-slice
  284.6 114.9 %all-reduce = bf16[512]{0:T(512)(128)(2,1)S(1)} all-reduce(bf16[512]{0:T(512)(128)(2,1)S(1)} %dynamic-update-slice), channel_id=2, replica_groups=mesh['seq'=64,'head'=8] {'seq'}, use_global_device_ids=true, to_apply=%add | all-reduce | flops 512 | bytes 2048
  399.6 2.2 reduce-window.6
  402.1 1.6 reshape.89
  403.7 33.8 %all-gather.10.cloned.1.call-done = bf16[512,64,128]{2,1,0:T(8,128)(2,1)} async-done(((bf16[8,64,128]{2,1,0:T(8,128)(2,1)}), bf16[512,64,128]{2,1,0:T(8,128)(2,1)}) %all-gather.10.cloned.1.call-update) | async-done | bytes 8388624 | tf_op jit(solution)/shard_map/all_gather | solution.py:31
  437.6 67.5 %while.28 = (s32[]{:T(128)}, f32[8,64,128]{2,1,0:T(8,128)S(1)}, s32[]{:T(128)}, bf16[64,8]{1,0:T(8,128)(2,1)S(1)}, bf16[64,8,64,128]{3,2,1,0:T(8,128)(2,1)}, /*index=5*/s32[]{:T(128)}, s32[]{:T(128)}) while((s32[]{:T(128)}, f32[8,64,128]{2,1,0:T(8,128)S(1)}, s32[]{:T(128)}, bf16[64,8]{1,0:T(8,128)(2,1)S(1)}, ...), condition=%wide.region_5.6_spmd.clone, body=%wide.region_4.5_spmd.clone.sunk | while | flops 327692 | bytes 655545 | solution.py:48
  437.6 1.0 fusion.93
  438.6 1.0 fusion.93
  439.7 1.0 fusion.93
  440.7 1.0 fusion.93
  441.8 1.0 fusion.93
  442.8 1.0 fusion.93
  443.9 1.0 fusion.93
  445.0 1.0 fusion.93
  446.0 1.0 fusion.93
  447.1 1.0 fusion.93
  448.1 1.0 fusion.93
  449.2 1.0 fusion.93
  450.2 1.0 fusion.93
  451.3 1.0 fusion.93
  452.3 1.0 fusion.93
  453.4 1.0 fusion.93
  454.5 1.0 fusion.93
  455.5 1.0 fusion.93
  459.7 1.0 fusion.93
  460.8 1.0 fusion.93
  464.0 1.0 fusion.93
  467.1 1.0 fusion.93
  468.2 1.0 fusion.93
  469.2 1.0 fusion.93
  472.4 1.0 fusion.93
  474.5 1.0 fusion.93
  476.6 1.0 fusion.93
  480.8 1.0 fusion.93
  484.0 1.0 fusion.93
  485.1 1.0 fusion.93
  490.3 1.0 fusion.93
  491.4 1.0 fusion.93
  495.6 1.0 fusion.93
  497.7 1.0 fusion.93
  498.8 1.0 fusion.93
  499.8 1.0 fusion.93
  503.0 1.0 fusion.93
  505.1 1.6 fusion.43
  507.0 73.6 %all-gather.8.cloned.1.call-done = bf16[4096,512]{1,0:T(8,128)(2,1)} async-done(((bf16[64,512]{1,0:T(8,128)(2,1)}), bf16[4096,512]{1,0:T(8,128)(2,1)}) %all-gather.8.cloned.1.call-update) | async-done | bytes 4194320 | tf_op jit(solution)/shard_map/all_gather | solution.py:116
  580.7 6.1 multiply_reduce_fusion
  586.7 21.6 %psum.7 = f32[512]{0:T(512)S(1)} all-reduce(f32[512]{0:T(512)S(1)} %get-tuple-element.267), channel_id=1, replica_groups=mesh['seq'=64,'head'=8] {'head'}, use_global_device_ids=true, to_apply=%region_9.10 | all-reduce | flops 512 | bytes 4096 | tf_op jit(solution)/shard_map/psum | solution.py:147
  (209 shorter events, 47.3 us)
Async XLA Ops:
  6.5 29.6 %copy-start.4 = (bf16[4096]{0:T(1024)(128)(2,1)S(1)}, bf16[4096]{0:T(1024)(128)(2,1)}, u32[]{:S(2)}) copy-start(bf16[4096]{0:T(1024)(128)(2,1)} %param.16) | copy-start | bytes 24580
  6.5 29.6 %copy-start.5 = (f32[4,512]{1,0:T(4,128)S(1)}, f32[4,512]{1,0:T(4,128)}, u32[]{:S(2)}) copy-start(f32[4,512]{1,0:T(4,128)} %param.20) | copy-start | bytes 24580
  9.2 214.5 %all-to-all-start = ((bf16[512,8,320]{2,1,0:T(8,128)(2,1)}), bf16[512,8,320]{2,1,0:T(8,128)(2,1)}, u32[]{:S(2)}, u32[]{:S(2)}) async-start(bf16[512,8,320]{2,1,0:T(8,128)(2,1)} %stack.2), calls=%async_computation | async-start | bytes 6291456 | tf_op jit(solution)/shard_map/all_to_all | solution.py:15
  35.3 175.9 %all-gather.6.cloned.1.call-start = ((), (), s32[]{:S(2)}) async-start(), calls=%async_computation.1 | async-start | bytes 4259840 | tf_op jit(solution)/shard_map/all_gather | solution.py:113
  36.1 401.5 %all-gather.10.cloned.1.call-start = ((), (), s32[]{:S(2)}) async-start(), calls=%async_computation.3 | async-start | bytes 8519680 | tf_op jit(solution)/shard_map/all_gather | solution.py:31
  36.2 187.6 %copy-start.2 = (f32[4096]{0:T(1024)}, f32[4096]{0:T(1024)S(1)}, u32[]{:S(2)}) copy-start(f32[4096]{0:T(1024)S(1)} %convert_element_type.78) | copy-start | bytes 49156
  36.2 184.0 %copy-start.6 = (f32[4,256]{1,0:T(4,128)S(1)}, f32[4,256]{1,0:T(4,128)}, u32[]{:S(2)}) copy-start(f32[4,256]{1,0:T(4,128)} %param.21) | copy-start | bytes 12292
  217.1 3.8 collective-permute-start
  223.7 8.9 %copy-start.8 = (f32[8]{0:T(128)S(1)}, f32[8]{0:T(128)}, u32[]{:S(2)}) copy-start(f32[8]{0:T(128)} %param.23) | copy-start | bytes 100
  223.7 8.9 %copy-start.9 = (f32[8]{0:T(128)S(1)}, f32[8]{0:T(128)}, u32[]{:S(2)}) copy-start(f32[8]{0:T(128)} %param.22) | copy-start | bytes 100
  228.5 6.9 %copy-start = (f32[4,128,8,64]{1,3,2,0:T(8,128)S(1)}, f32[4,128,8,64]{1,3,2,0:T(8,128)}, u32[]{:S(2)}) copy-start(f32[4,128,8,64]{1,3,2,0:T(8,128)} %copy.51) | copy-start | bytes 3145732
  228.6 5.1 collective-permute-start.1
  234.5 0.7 copy-start.1
  280.4 224.7 %copy-start.10 = (f32[8]{0:T(128)S(1)}, f32[8]{0:T(128)}, u32[]{:S(2)}) copy-start(f32[8]{0:T(128)} %param.24) | copy-start | bytes 100
  281.2 299.5 %all-gather.8.cloned.1.call-start = ((), (), s32[]{:S(2)}) async-start(), calls=%async_computation.2 | async-start | bytes 4259840 | tf_op jit(solution)/shard_map/all_gather | solution.py:116
  437.6 143.1 %copy-start.3 = (f32[4096]{0:T(1024)S(1)}, f32[4096]{0:T(1024)}, u32[]{:S(2)}) copy-start(f32[4096]{0:T(1024)} %copy-done.2) | copy-start | bytes 49156
  507.0 101.3 %copy-start.7 = (f32[512]{0:T(512)S(1)}, f32[512]{0:T(512)}, u32[]{:S(2)}) copy-start(f32[512]{0:T(512)} %param.25) | copy-start | bytes 6148
Sparse Core Ops, SparseCore 0:
  39.1 172.1 all-gather.5
  281.3 156.2 all-gather.9
  440.5 140.1 all-gather.7
